TPU v7x, 32 devices: a whole 2x2x4 slice. The times are simulated.
32 devices in a mesh: old: 4 (over y, core), new: 8 (over z, x).
Axes of the slice: x: 2, y: 2, z: 4, core: 2. Of those that a mesh axis runs over, the one named last changes fastest.
Arguments:
- old_field: bfloat16 [3, 27, 98304], P(None, None, ('old', 'new')), may hold values from -6 to 6
- pair_dest: int32 [32768, 1], P(('old', 'new')), may hold values from 0 to 31; in each aligned block of 1024 rows (0 to 1023, 1024 to 2047, ...) at most 128 rows name the same one
- pair_new: int32 [32768], P(('old', 'new')), may hold values from 0 to 511
- pair_old: int32 [32768], P(('old', 'new')), may hold values from 0 to 3071
- pair_block: int32 [32768], P(('old', 'new')), may hold values from 0 to 3
- basis_old: bfloat16 [4, 27, 125], replicated, may hold values from -1.25 to 1.25
- basis_new: bfloat16 [4, 27, 125], replicated, may hold values from -0.5 to 0.5
- volume: float32 [2, 8, 1024], P(None, 'old', 'new'), may hold values from 0.25 to 36, as said below
Outputs:
- solution: float32 [3, 5, 16, 2048], P(None, None, 'old', 'new')
- residual: float32 [3, 5, 16, 2048], P(None, None, 'old', 'new')
Inputs may be any that keep to these rules, and one draw needn't show every extreme that they name: `pair_dest`: a device's index is its position along old times the number of devices along new plus its position along new; in each device's block of 1024 pairs at most 128 name one destination. `pair_new`: local element number (x * 2 + y) * 128 + z within the destination's block. `pair_old`: old element within the block of the device that holds the pair. `volume`: positive element factors.
All inputs are finite; a program needn't handle non-finite values.
Results may differ from a plain program's by a relative error of at most 0.003.
Values may be sent and summed in bfloat16 or wider, within the bound.
A program may use at most 64 MiB of HBM per device.

v0:
```python
import jax
import jax.numpy as jnp
import numpy as np
from jax import lax
from jax.sharding import PartitionSpec as P

ITERS = 4
LINE_MASS = np.array([[4.0, 2.0, -1.0], [2.0, 16.0, 2.0], [-1.0, 2.0, 4.0]]) / 15.0


def passed_along(shard, axis, by):
    size = lax.axis_size(axis)
    return lax.ppermute(shard, axis, [(i, (i + by) % size) for i in range(size)])


def split_axis(array, axis, count):
    moved = jnp.moveaxis(array, axis, -1)
    paired = moved[..., : 2 * count].reshape(moved.shape[:-1] + (count, 2))
    even_nodes = paired[..., 0]
    odd_nodes = paired[..., 1]
    after_nodes = jnp.concatenate(
        [even_nodes[..., 1:], moved[..., 2 * count : 2 * count + 1]], axis=-1
    )
    stacked = jnp.stack([even_nodes, odd_nodes, after_nodes], axis=0)
    return jnp.moveaxis(stacked, -1, axis + 1)


def pick_nodes(extended, cell_counts):
    along_first, along_second, along_third = cell_counts
    stacked = split_axis(extended, 3, along_third)
    stacked = split_axis(stacked, 3, along_second)
    stacked = split_axis(stacked, 3, along_first)
    return jnp.transpose(stacked, (3, 0, 1, 2, 4, 5, 6))


def merge_axis(array, local_axis, cell_axis):
    moved = jnp.moveaxis(array, (local_axis, cell_axis), (0, -1))
    count = moved.shape[-1]
    zero_pad = [(0, 0)] * (moved.ndim - 2)
    even_full = jnp.pad(moved[0], zero_pad + [(0, 1)]) + jnp.pad(moved[2], zero_pad + [(1, 0)])
    woven = jnp.stack([even_full[..., :count], moved[1]], axis=-1)
    woven = woven.reshape(woven.shape[:-2] + (2 * count,))
    return jnp.concatenate([woven, even_full[..., count:]], axis=-1)


def spread_nodes(element_nodes):
    summed = merge_axis(element_nodes, 3, 6)
    summed = merge_axis(summed, 2, 4)
    summed = merge_axis(summed, 1, 2)
    return jnp.transpose(summed, (0, 3, 2, 1))


def element_mass(element_nodes, volume):
    line_mass = jnp.asarray(LINE_MASS, dtype=jnp.float32)
    high = lax.Precision.HIGHEST
    applied = jnp.einsum("ia,cabdxyz->cibdxyz", line_mass, element_nodes, precision=high)
    applied = jnp.einsum("jb,cibdxyz->cijdxyz", line_mass, applied, precision=high)
    applied = jnp.einsum("kd,cijdxyz->cijkxyz", line_mass, applied, precision=high)
    return applied * volume


def fold_rims(assembled):
    front_face = passed_along(assembled[..., -1], "new", 1)
    inner_part = assembled[..., :-1]
    inner_part = jnp.concatenate(
        [inner_part[..., :1] + front_face[..., None], inner_part[..., 1:]], axis=3
    )
    side_face = passed_along(inner_part[:, :, -1, :], "old", 1)
    folded = inner_part[:, :, :-1]
    folded = jnp.concatenate(
        [folded[:, :, :1] + side_face[:, :, None, :], folded[:, :, 1:]], axis=2
    )
    return folded


def operate(vector, volume):
    upper_layer = passed_along(vector[..., 0], "new", -1)
    extended = jnp.concatenate([vector, upper_layer[..., None]], axis=3)
    upper_row = passed_along(extended[:, :, 0, :], "old", -1)
    extended = jnp.concatenate([extended, upper_row[:, :, None, :]], axis=2)
    element_nodes = pick_nodes(extended, volume.shape)
    return fold_rims(spread_nodes(element_mass(element_nodes, volume)))


def quadrature(coefficients, block_kind, basis_old, basis_new):
    summed = jnp.zeros(coefficients.shape, jnp.float32)
    for q in range(basis_old.shape[0]):
        chosen = jnp.where(
            (block_kind == q)[None, None, :], coefficients, jnp.zeros((), coefficients.dtype)
        )
        values = jnp.einsum(
            "cap,ak->ckp", chosen, basis_old[q], preferred_element_type=jnp.float32
        ).astype(jnp.bfloat16)
        summed = summed + jnp.einsum(
            "ckp,ak->cap", values, basis_new[q], preferred_element_type=jnp.float32
        )
    return summed


def squares(residual):
    return lax.psum(jnp.sum(residual * residual, axis=(1, 2, 3)), ("old", "new"))


def on_device(old_field, pair_dest, pair_new, pair_old, pair_block, basis_old, basis_new, volume):
    devices = lax.axis_size(("old", "new"))
    pair_count = pair_dest.shape[0]
    capacity = 4 * pair_count // devices
    cells_one, cells_two, cells_three = volume.shape
    elements = cells_one * cells_two * cells_three
    destination = pair_dest[:, 0]
    onehot = (destination[:, None] == jnp.arange(devices, dtype=jnp.int32)[None, :]).astype(
        jnp.int32
    )
    slot_rank = jnp.sum((jnp.cumsum(onehot, axis=0) - onehot) * onehot, axis=1)
    position = destination * capacity + slot_rank
    gathered = jnp.take(old_field, pair_old, axis=2)
    contribution = quadrature(gathered, pair_block, basis_old, basis_new)
    outgoing = (
        jnp.zeros((81, devices * capacity), jnp.float32)
        .at[:, position]
        .set(contribution.reshape(81, -1))
    )
    targets = jnp.full((devices * capacity,), elements, jnp.int32).at[position].set(pair_new)
    received, slot_element = (
        lax.all_to_all(
            outgoing.reshape(81, devices, capacity),
            ("old", "new"),
            split_axis=1,
            concat_axis=1,
            tiled=True,
        ),
        lax.all_to_all(
            targets.reshape(1, devices, capacity),
            ("old", "new"),
            split_axis=1,
            concat_axis=1,
            tiled=True,
        ),
    )
    arrived = received.reshape(81, -1)
    slot_element = slot_element.reshape(-1)
    element_load = (
        jnp.zeros((81, elements + 1), jnp.float32).at[:, slot_element].add(arrived)[:, :elements]
    )
    load_vector = fold_rims(
        spread_nodes(element_load.reshape(3, 3, 3, 3, cells_one, cells_two, cells_three))
    )
    solution = jnp.zeros_like(load_vector)
    residual = load_vector
    direction = load_vector
    norm_now = squares(residual)
    for iteration in range(ITERS):
        applied = operate(direction, volume)
        curvature = lax.psum(jnp.sum(direction * applied, axis=(1, 2, 3)), ("old", "new"))
        step_size = norm_now / curvature
        solution = solution + step_size[:, None, None, None] * direction
        residual = residual - step_size[:, None, None, None] * applied
        norm_next = squares(residual)
        direction = residual + (norm_next / norm_now)[:, None, None, None] * direction
        norm_now = norm_next
    return (solution, residual)


def solution(mesh):
    in_specs = (
        P(None, None, ("old", "new")),
        P(("old", "new"), None),
        P(("old", "new")),
        P(("old", "new")),
        P(("old", "new")),
        P(),
        P(),
        P(None, "old", "new"),
    )
    out_specs = (P(None, None, "old", "new"), P(None, None, "old", "new"))
    return jax.shard_map(
        on_device, mesh=mesh, in_specs=in_specs, out_specs=out_specs, check_vma=False
    )
```

profile of v0, /device:TPU:10, one launch (start us, length us, event | category | flops | bytes accessed | tf_op | source)
XLA Modules:
  0.0 578.3 jit_solution(5909297454449030575)
XLA Ops:
  1.3 9.0 %reduce-window.6 = s32[32,8,128]{2,1,0:T(8,128)S(1)} reduce-window(s32[32,8,128]{2,1,0:T(8,128)S(1)} %fusion.60, s32[]{:T(128)} %constant.17.clone.1), window={size=1x1x128 pad=0_0x0_0x127_0}, to_apply=%region_0.0 | reduce-window | flops 4161536 | bytes 262148 | tf_op jit(solution)/shard_map/reduce-window
  10.8 0.7 fusion.59
  12.3 5.1 scatter_custom_fusion
  17.3 6.0 %all-to-all-start = ((s32[1,32,128]{2,0,1:T(1,128)}), s32[1,32,128]{2,0,1:T(1,128)S(1)}, u32[]{:S(2)}, u32[]{:S(2)}) async-start(s32[1,32,128]{2,0,1:T(1,128)} %bitcast.6), calls=%async_computation | async-start | bytes 32768 | tf_op jit(solution)/shard_map/all_to_all | solution.py:132
  24.0 0.7 broadcast_compare_fusion.3
  24.8 4.5 copy.623
  30.0 7.5 %gather_fusion = bf16[1024,3,27]{2,1,0:T(4,128)(2,1)} fusion(bf16[3,27,3072]{1,0,2:T(4,128)(2,1)S(1)} %copy.623, s32[1024]{0:T(1024)S(1)} %fusion.106), kind=kCustom, calls=%fused_computation | custom fusion | bytes 335872 | tf_op jit(solution)/shard_map/jit(_take)/gather | solution.py:116
  37.6 9.2 %select_bitcast_fusion.3 = (bf16[3,27,1024]{1,0,2:T(4,128)(2,1)}, bf16[3,27,1024]{1,0,2:T(4,128)(2,1)S(1)}, bf16[3,27,1024]{1,0,2:T(4,128)(2,1)S(1)}, bf16[3,27,1024]{1,0,2:T(4,128)(2,1)S(1)}) fusion(pred[1024]{0:T(1024)(128)(4,1)S(1)} %get-tuple-element.120, bf16[1024,3,27]{2,1,0:T(4,128)(2,1)} %gather_fusion, pred[1024]{0:T(1024)(128)(4,1)S(1)} %get-tuple-element.126, ...), kind=kLoop, calls=%fused_computation.31 | loop fusion | flops 414720 | bytes 834560 | tf_op jit(solution)/shard_map/jit(_where)/select_n | solution.py:88
  46.8 1.4 fusion.6
  48.2 2.3 fusion.5
  50.4 1.4 fusion.4
  51.8 1.7 fusion.11
  53.8 3.8 scatter_custom_fusion.1
  57.6 1.8 copy.641
  59.3 5.8 %all-to-all-start.1 = ((f32[81,32,128]{2,0,1:T(8,128)}), f32[81,32,128]{2,0,1:T(8,128)S(1)}, u32[]{:S(2)}, u32[]{:S(2)}) async-start(f32[81,32,128]{2,0,1:T(8,128)} %copy.641), calls=%async_computation.1 | async-start | bytes 2883584 | tf_op jit(solution)/shard_map/all_to_all | solution.py:125
  65.8 31.4 %all-to-all-done.1 = f32[81,32,128]{2,0,1:T(8,128)S(1)} async-done(((f32[81,32,128]{2,0,1:T(8,128)}), f32[81,32,128]{2,0,1:T(8,128)S(1)}, u32[]{:S(2)}, u32[]{:S(2)}) %all-to-all-start.1) | async-done | bytes 1327136 | tf_op jit(solution)/shard_map/all_to_all | solution.py:125
  97.6 1.0 copy.830
  98.6 0.8 copy.643
  99.4 28.0 %scatter_custom_fusion.2 = f32[81,513]{0,1:T(8,128)S(1)} fusion(s32[4096]{0:T(1024)} %bitcast.616, f32[4096,81]{1,0:T(8,128)S(1)} %copy.643, f32[]{:T(128)} %constant.14.clone.1), kind=kCustom, calls=%fused_computation.113 | custom fusion | flops 331776 | bytes 166724 | tf_op jit(solution)/shard_map/scatter-add | solution.py:143
  128.1 4.3 copy.777
  132.4 6.2 %reshape.241 = f32[3,3,3,2,2,256]{5,4,3,0,1,2:T(2,128)S(1)} reshape(f32[3,3,3,2,2,128,2]{6,5,4,3,0,1,2:T(8,128)} %copy.777) | data formatting | bytes 221184 | tf_op jit(solution)/shard_map/reshape | solution.py:42
  140.1 3.0 collective-permute-done
  143.7 3.0 collective-permute-done.1
  147.0 2.4 collective-permute-start.2
  149.4 2.1 collective-permute-done.2
  151.8 1.6 collective-permute-done.3
  154.1 2.5 fusion.118
  156.6 2.2 copy.806
  162.4 4.3 copy.779
  166.7 6.2 %reshape.242 = f32[3,3,3,2,2,256]{5,4,3,0,1,2:T(2,128)S(1)} reshape(f32[3,3,3,2,2,128,2]{6,5,4,3,0,1,2:T(8,128)} %copy.779) | data formatting | bytes 221184 | tf_op jit(solution)/shard_map/reshape | solution.py:42
  174.5 3.0 collective-permute-done.4
  178.1 2.9 collective-permute-done.5
  181.4 45.8 %all-reduce.30 = (f32[3]{0:T(128)S(1)}, f32[3]{0:T(128)S(1)}) all-reduce(f32[3]{0:T(128)S(1)} %get-tuple-element.7, f32[3]{0:T(128)S(1)} %get-tuple-element.6), channel_id=1, replica_groups=mesh['old'=4,'new'=8] {'old','new'}, use_global_device_ids=true, to_apply=%region_7.8 | all-reduce | flops 6 | bytes 48 | tf_op jit(solution)/shard_map/psum | solution.py:101
  227.4 38.4 %psum.58 = f32[3]{0:T(128)S(1)} all-reduce(f32[3]{0:T(128)S(1)} %get-tuple-element.20), channel_id=1, replica_groups=mesh['old'=4,'new'=8] {'old','new'}, use_global_device_ids=true, to_apply=%region_11.12 | all-reduce | flops 3 | bytes 24 | tf_op jit(solution)/shard_map/psum | solution.py:101
  266.2 4.5 collective-permute-done.6
  271.2 1.6 collective-permute-done.7
  273.4 2.5 fusion.117
  275.9 2.2 copy.812
  281.7 4.3 copy.781
  286.0 6.2 %reshape.243 = f32[3,3,3,2,2,256]{5,4,3,0,1,2:T(2,128)S(1)} reshape(f32[3,3,3,2,2,128,2]{6,5,4,3,0,1,2:T(8,128)} %copy.781) | data formatting | bytes 221184 | tf_op jit(solution)/shard_map/reshape | solution.py:42
  293.2 3.6 collective-permute-done.8
  297.5 2.8 collective-permute-done.9
  300.6 42.8 %psum.59 = f32[3]{0:T(128)S(1)} all-reduce(f32[3]{0:T(128)S(1)} %get-tuple-element.18), channel_id=1, replica_groups=mesh['old'=4,'new'=8] {'old','new'}, use_global_device_ids=true, to_apply=%region_13.14 | all-reduce | flops 3 | bytes 24 | tf_op jit(solution)/shard_map/psum | solution.py:154
  343.6 39.3 %psum.60 = f32[3]{0:T(128)S(1)} all-reduce(f32[3]{0:T(128)S(1)} %get-tuple-element.16), channel_id=1, replica_groups=mesh['old'=4,'new'=8] {'old','new'}, use_global_device_ids=true, to_apply=%region_15.16 | all-reduce | flops 3 | bytes 24 | tf_op jit(solution)/shard_map/psum | solution.py:101
  383.2 4.5 collective-permute-done.10
  388.4 1.6 collective-permute-done.11
  390.7 2.5 fusion.116
  393.1 2.2 copy.818
  399.0 4.3 copy.783
  403.3 6.2 %reshape.244 = f32[3,3,3,2,2,256]{5,4,3,0,1,2:T(2,128)S(1)} reshape(f32[3,3,3,2,2,128,2]{6,5,4,3,0,1,2:T(8,128)} %copy.783) | data formatting | bytes 221184 | tf_op jit(solution)/shard_map/reshape | solution.py:42
  410.4 3.6 collective-permute-done.12
  414.4 3.2 collective-permute-done.13
  417.9 42.8 %psum.61 = f32[3]{0:T(128)S(1)} all-reduce(f32[3]{0:T(128)S(1)} %get-tuple-element.14), channel_id=1, replica_groups=mesh['old'=4,'new'=8] {'old','new'}, use_global_device_ids=true, to_apply=%region_17.18 | all-reduce | flops 3 | bytes 24 | tf_op jit(solution)/shard_map/psum | solution.py:154
  460.9 38.9 %psum.62 = f32[3]{0:T(128)S(1)} all-reduce(f32[3]{0:T(128)S(1)} %get-tuple-element.12), channel_id=1, replica_groups=mesh['old'=4,'new'=8] {'old','new'}, use_global_device_ids=true, to_apply=%region_19.20 | all-reduce | flops 3 | bytes 24 | tf_op jit(solution)/shard_map/psum | solution.py:101
  500.1 4.5 collective-permute-done.14
  505.0 1.6 collective-permute-done.15
  507.3 2.5 fusion.115
  509.8 2.2 copy.824
  515.6 4.3 copy.785
  519.9 6.2 %reshape.245 = f32[3,3,3,2,2,256]{5,4,3,0,1,2:T(2,128)S(1)} reshape(f32[3,3,3,2,2,128,2]{6,5,4,3,0,1,2:T(8,128)} %copy.785) | data formatting | bytes 221184 | tf_op jit(solution)/shard_map/reshape | solution.py:42
  527.1 3.6 collective-permute-done.16
  531.1 3.1 collective-permute-done.17
  534.5 42.8 %psum.63 = f32[3]{0:T(128)S(1)} all-reduce(f32[3]{0:T(128)S(1)} %get-tuple-element.10), channel_id=1, replica_groups=mesh['old'=4,'new'=8] {'old','new'}, use_global_device_ids=true, to_apply=%region_21.22 | all-reduce | flops 3 | bytes 24 | tf_op jit(solution)/shard_map/psum | solution.py:154
  577.3 0.8 multiply_subtract_fusion
  (333 shorter events, 34.3 us)
Async XLA Ops:
  10.8 18.5 %copy-start.2 = (bf16[4,27,125]{2,0,1:T(4,128)(2,1)S(1)}, bf16[4,27,125]{2,0,1:T(4,128)(2,1)}, u32[]{:S(2)}) copy-start(bf16[4,27,125]{2,0,1:T(4,128)(2,1)} %param.17) | copy-start | bytes 81004
  10.8 18.5 %copy-start.3 = (bf16[4,27,125]{2,0,1:T(4,128)(2,1)S(1)}, bf16[4,27,125]{2,0,1:T(4,128)(2,1)}, u32[]{:S(2)}) copy-start(bf16[4,27,125]{2,0,1:T(4,128)(2,1)} %param.18) | copy-start | bytes 81004
  12.3 11.8 %copy-start.5 = (s32[1024,1]{0,1:T(1,128)}, s32[1024,1]{0,1:T(1,128)S(1)}, u32[]{:S(2)}) copy-start(s32[1024,1]{0,1:T(1,128)S(1)} %compare_select_fusion.1) | copy-start | bytes 12292
  17.3 42.0 %all-to-all-start = ((s32[1,32,128]{2,0,1:T(1,128)}), s32[1,32,128]{2,0,1:T(1,128)S(1)}, u32[]{:S(2)}, u32[]{:S(2)}) async-start(s32[1,32,128]{2,0,1:T(1,128)} %bitcast.6), calls=%async_computation | async-start | bytes 32768 | tf_op jit(solution)/shard_map/all_to_all | solution.py:132
  48.2 3.6 copy-start
  59.3 37.9 %all-to-all-start.1 = ((f32[81,32,128]{2,0,1:T(8,128)}), f32[81,32,128]{2,0,1:T(8,128)S(1)}, u32[]{:S(2)}, u32[]{:S(2)}) async-start(f32[81,32,128]{2,0,1:T(8,128)} %copy.641), calls=%async_computation.1 | async-start | bytes 2883584 | tf_op jit(solution)/shard_map/all_to_all | solution.py:125
  139.4 3.7 collective-permute-start
  143.4 3.3 collective-permute-start.1
  147.0 4.6 collective-permute-start.2
  151.7 1.6 collective-permute-start.3
  158.8 1.5 copy-start.1
  159.6 2.4 copy-start.4
  173.8 3.7 collective-permute-start.4
  177.8 3.3 collective-permute-start.5
  266.1 4.6 collective-permute-start.6
  270.9 1.8 collective-permute-start.7
  293.1 3.7 collective-permute-start.8
  297.1 3.3 collective-permute-start.9
  383.2 4.6 collective-permute-start.10
  387.9 2.0 collective-permute-start.11
  410.3 3.7 collective-permute-start.12
  414.3 3.3 collective-permute-start.13
  500.0 4.6 collective-permute-start.14
  504.8 1.8 collective-permute-start.15
  526.9 3.7 collective-permute-start.16
  530.9 3.3 collective-permute-start.17
where the time goes:
time: 588 us; the launch traced here: 578 us
  blocking collectives  291 us (49%)
  local copies, waits for them, and re-layouts  109 us (19%)
  waiting for transfers between devices  85.1 us (14%)
  other arithmetic  59.1 us (10%)
  starting transfers between devices  17.8 us (3%)
  matrix products  13.5 us (2%)
    psum x4, blocking collectives, squares(): lax.psum(jnp.sum(residual * residual, axis=(1, 2, 3)), ('old', 'new'))  162 us
    psum x3, blocking collectives, on_device(): lax.psum(jnp.sum(direction * applied, axis=(1, 2, 3)), ('old', 'new'))  128 us
    ppermute x18, waiting for transfers between devices, passed_along(): lax.ppermute(shard, axis, [(i, (i + by) % size) for i in range(size)])  53.7 us
    reshape x20, local copies, waits for them, and re-layouts, merge_axis(): woven = woven.reshape(woven.shape[:-2] + (2 * count,))  52.6 us
    all_to_all x1, waiting for transfers between devices, on_device(): lax.all_to_all(outgoing.reshape(81, devices, capacity), ('old', 'new'), s...  31.4 us
    scatter-add x1, other arithmetic, on_device(): jnp.zeros((81, elements + 1), jnp.float32).at[:, slot_element].add(arrived)  28 us
    unnamed x39, local copies, waits for them, and re-layouts  16.9 us
  transfers between devices with their start and end apart: 20, of which 19 were waited for; matrix products, arithmetic and copies ran while one was open for 6% of the time, Pallas kernels for 0%

commit v1 on v0

--- a/solution.py
+++ b/solution.py
@@ -122,12 +122,20 @@
     )
     targets = jnp.full((devices * capacity,), elements, jnp.int32).at[position].set(pair_new)
     received, slot_element = (
-        lax.all_to_all(
-            outgoing.reshape(81, devices, capacity),
-            ("old", "new"),
-            split_axis=1,
-            concat_axis=1,
-            tiled=True,
+        jnp.concatenate(
+            lax.all_to_all(
+                jnp.stack(
+                    jnp.split(
+                        outgoing.reshape(81, devices, capacity),
+                        lax.axis_size(("old", "new")),
+                        axis=1,
+                    )
+                ),
+                ("old", "new"),
+                0,
+                0,
+            ),
+            axis=1,
         ),
         lax.all_to_all(
             targets.reshape(1, devices, capacity),

time: 588 us -> 615 us (1.046)
  local copies, waits for them, and re-layouts: 109 us -> 139 us
    unnamed x39 -> x108, local copies, waits for them, and re-layouts: 16.9 us -> 47.7 us
  transfers between devices with their start and end apart: 20 -> 20, of which waited for: 19 -> 19; matrix products, arithmetic and copies ran while one was open for 6% -> 11% of each run, Pallas kernels for 0% -> 0%
where the time goes in v1:
time: 615 us; the launch traced here: 605 us
  blocking collectives  291 us (47%)
  local copies, waits for them, and re-layouts  139 us (23%)
  waiting for transfers between devices  83.4 us (14%)
  other arithmetic  57.9 us (9%)
  starting transfers between devices  17.1 us (3%)
  matrix products  13.3 us (2%)
    psum x4, blocking collectives, squares(): lax.psum(jnp.sum(residual * residual, axis=(1, 2, 3)), ('old', 'new'))  162 us
    psum x3, blocking collectives, on_device(): lax.psum(jnp.sum(direction * applied, axis=(1, 2, 3)), ('old', 'new'))  128 us
    ppermute x18, waiting for transfers between devices, passed_along(): lax.ppermute(shard, axis, [(i, (i + by) % size) for i in range(size)])  54.3 us
    reshape x20, local copies, waits for them, and re-layouts, merge_axis(): woven = woven.reshape(woven.shape[:-2] + (2 * count,))  52.6 us
    unnamed x108, local copies, waits for them, and re-layouts  47.7 us
    all_to_all x1, waiting for transfers between devices, on_device(): lax.all_to_all(jnp.stack(jnp.split(outgoing.reshape(81, devices, capacity...  29.1 us
    scatter-add x1, other arithmetic, on_device(): jnp.zeros((81, elements + 1), jnp.float32).at[:, slot_element].add(arrived)  28.1 us
  transfers between devices with their start and end apart: 20, of which 19 were waited for; matrix products, arithmetic and copies ran while one was open for 11% of the time, Pallas kernels for 0%

profile of v1, /device:TPU:10, one launch (start us, length us, event | category | flops | bytes accessed | tf_op | source)
XLA Modules:
  0.0 605.0 jit_solution(4327116500128814933)
XLA Ops:
  1.4 9.0 %reduce-window.6 = s32[32,8,128]{2,1,0:T(8,128)S(1)} reduce-window(s32[32,8,128]{2,1,0:T(8,128)S(1)} %fusion.60, s32[]{:T(128)} %constant.17.clone.1), window={size=1x1x128 pad=0_0x0_0x127_0}, to_apply=%region_0.0 | reduce-window | flops 4161536 | bytes 262148 | tf_op jit(solution)/shard_map/reduce-window
  12.3 5.1 scatter_custom_fusion
  17.3 6.0 all-to-all-start
  23.4 4.5 copy.654
  28.7 7.5 %gather_fusion = bf16[1024,3,27]{2,1,0:T(4,128)(2,1)} fusion(bf16[3,27,3072]{1,0,2:T(4,128)(2,1)S(1)} %copy.654, s32[1024]{0:T(1024)S(1)} %fusion.106), kind=kCustom, calls=%fused_computation | custom fusion | bytes 335872 | tf_op jit(solution)/shard_map/jit(_take)/gather | solution.py:116
  36.2 9.2 %select_bitcast_fusion.3 = (bf16[3,27,1024]{1,0,2:T(4,128)(2,1)}, bf16[3,27,1024]{1,0,2:T(4,128)(2,1)S(1)}, bf16[3,27,1024]{1,0,2:T(4,128)(2,1)S(1)}, bf16[3,27,1024]{1,0,2:T(4,128)(2,1)S(1)}) fusion(pred[1024]{0:T(1024)(128)(4,1)S(1)} %get-tuple-element.152, bf16[1024,3,27]{2,1,0:T(4,128)(2,1)} %gather_fusion, pred[1024]{0:T(1024)(128)(4,1)S(1)} %get-tuple-element.158, ...), kind=kLoop, calls=%fused_computation.32 | loop fusion | flops 414720 | bytes 834560 | tf_op jit(solution)/shard_map/jit(_where)/select_n | solution.py:88
  45.4 1.4 fusion.6
  46.8 2.3 fusion.5
  49.1 1.4 fusion.4
  50.6 1.4 fusion.11
  52.2 3.8 scatter_custom_fusion.1
  57.0 0.9 copy.879
  58.0 0.9 copy.878
  59.9 0.9 copy.876
  62.7 0.9 copy.873
  65.5 0.9 copy.870
  88.3 5.8 all-to-all-start.1
  94.8 29.1 %all-to-all-done.1 = f32[32,81,1,128]{3,2,1,0:T(1,128)S(1)} async-done(((f32[32,81,1,128]{3,2,1,0:T(1,128)}), f32[32,81,1,128]{3,2,1,0:T(1,128)S(1)}, u32[]{:S(2)}, u32[]{:S(2)}) %all-to-all-start.1) | async-done | bytes 1327136 | tf_op jit(solution)/shard_map/all_to_all | solution.py:126
  124.2 1.0 copy.924
  126.1 28.1 %scatter_custom_fusion.2 = f32[81,513]{0,1:T(8,128)S(1)} fusion(s32[4096]{0:T(1024)} %bitcast.688, f32[4096,81]{1,0:T(8,128)S(1)} %copy.705, f32[]{:T(128)} %constant.14.clone.1), kind=kCustom, calls=%fused_computation.114 | custom fusion | flops 331776 | bytes 166724 | tf_op jit(solution)/shard_map/scatter-add | solution.py:151
  154.9 4.3 copy.839
  159.2 6.2 %reshape.241 = f32[3,3,3,2,2,256]{5,4,3,0,1,2:T(2,128)S(1)} reshape(f32[3,3,3,2,2,128,2]{6,5,4,3,0,1,2:T(8,128)} %copy.839) | data formatting | bytes 221184 | tf_op jit(solution)/shard_map/reshape | solution.py:42
  166.8 3.2 collective-permute-done
  170.5 3.0 collective-permute-done.1
  173.8 2.2 collective-permute-start.2
  176.1 2.3 collective-permute-done.2
  178.7 1.6 collective-permute-done.3
  181.0 2.5 fusion.120
  183.4 2.2 copy.900
  189.3 4.3 copy.841
  193.6 6.2 %reshape.242 = f32[3,3,3,2,2,256]{5,4,3,0,1,2:T(2,128)S(1)} reshape(f32[3,3,3,2,2,128,2]{6,5,4,3,0,1,2:T(8,128)} %copy.841) | data formatting | bytes 221184 | tf_op jit(solution)/shard_map/reshape | solution.py:42
  201.1 3.2 collective-permute-done.4
  205.0 3.0 collective-permute-done.5
  208.2 45.6 %all-reduce.30 = (f32[3]{0:T(128)S(1)}, f32[3]{0:T(128)S(1)}) all-reduce(f32[3]{0:T(128)S(1)} %get-tuple-element.7, f32[3]{0:T(128)S(1)} %get-tuple-element.6), channel_id=1, replica_groups=mesh['old'=4,'new'=8] {'old','new'}, use_global_device_ids=true, to_apply=%region_7.8 | all-reduce | flops 6 | bytes 48 | tf_op jit(solution)/shard_map/psum | solution.py:101
  254.1 38.4 %psum.58 = f32[3]{0:T(128)S(1)} all-reduce(f32[3]{0:T(128)S(1)} %get-tuple-element.20), channel_id=1, replica_groups=mesh['old'=4,'new'=8] {'old','new'}, use_global_device_ids=true, to_apply=%region_11.12 | all-reduce | flops 3 | bytes 24 | tf_op jit(solution)/shard_map/psum | solution.py:101
  292.8 4.5 collective-permute-done.6
  297.8 1.6 collective-permute-done.7
  300.0 2.5 fusion.119
  302.5 2.2 copy.906
  308.3 4.3 copy.843
  312.6 6.2 %reshape.243 = f32[3,3,3,2,2,256]{5,4,3,0,1,2:T(2,128)S(1)} reshape(f32[3,3,3,2,2,128,2]{6,5,4,3,0,1,2:T(8,128)} %copy.843) | data formatting | bytes 221184 | tf_op jit(solution)/shard_map/reshape | solution.py:42
  319.8 3.6 collective-permute-done.8
  324.1 2.9 collective-permute-done.9
  327.2 42.8 %psum.59 = f32[3]{0:T(128)S(1)} all-reduce(f32[3]{0:T(128)S(1)} %get-tuple-element.18), channel_id=1, replica_groups=mesh['old'=4,'new'=8] {'old','new'}, use_global_device_ids=true, to_apply=%region_13.14 | all-reduce | flops 3 | bytes 24 | tf_op jit(solution)/shard_map/psum | solution.py:162
  370.2 39.3 %psum.60 = f32[3]{0:T(128)S(1)} all-reduce(f32[3]{0:T(128)S(1)} %get-tuple-element.16), channel_id=1, replica_groups=mesh['old'=4,'new'=8] {'old','new'}, use_global_device_ids=true, to_apply=%region_15.16 | all-reduce | flops 3 | bytes 24 | tf_op jit(solution)/shard_map/psum | solution.py:101
  409.8 4.5 collective-permute-done.10
  414.8 1.6 collective-permute-done.11
  417.1 2.5 fusion.118
  419.5 2.2 copy.912
  425.4 4.3 copy.845
  429.6 6.2 %reshape.244 = f32[3,3,3,2,2,256]{5,4,3,0,1,2:T(2,128)S(1)} reshape(f32[3,3,3,2,2,128,2]{6,5,4,3,0,1,2:T(8,128)} %copy.845) | data formatting | bytes 221184 | tf_op jit(solution)/shard_map/reshape | solution.py:42
  436.8 3.6 collective-permute-done.12
  440.8 3.2 collective-permute-done.13
  444.3 42.8 %psum.61 = f32[3]{0:T(128)S(1)} all-reduce(f32[3]{0:T(128)S(1)} %get-tuple-element.14), channel_id=1, replica_groups=mesh['old'=4,'new'=8] {'old','new'}, use_global_device_ids=true, to_apply=%region_17.18 | all-reduce | flops 3 | bytes 24 | tf_op jit(solution)/shard_map/psum | solution.py:162
  487.3 38.9 %psum.62 = f32[3]{0:T(128)S(1)} all-reduce(f32[3]{0:T(128)S(1)} %get-tuple-element.12), channel_id=1, replica_groups=mesh['old'=4,'new'=8] {'old','new'}, use_global_device_ids=true, to_apply=%region_19.20 | all-reduce | flops 3 | bytes 24 | tf_op jit(solution)/shard_map/psum | solution.py:101
  526.5 4.5 collective-permute-done.14
  531.5 1.6 collective-permute-done.15
  533.8 2.5 fusion.117
  536.2 2.2 copy.918
  542.1 4.3 copy.847
  546.3 6.2 %reshape.245 = f32[3,3,3,2,2,256]{5,4,3,0,1,2:T(2,128)S(1)} reshape(f32[3,3,3,2,2,128,2]{6,5,4,3,0,1,2:T(8,128)} %copy.847) | data formatting | bytes 221184 | tf_op jit(solution)/shard_map/reshape | solution.py:42
  553.5 3.6 collective-permute-done.16
  557.6 3.1 collective-permute-done.17
  561.0 42.8 %psum.63 = f32[3]{0:T(128)S(1)} all-reduce(f32[3]{0:T(128)S(1)} %get-tuple-element.10), channel_id=1, replica_groups=mesh['old'=4,'new'=8] {'old','new'}, use_global_device_ids=true, to_apply=%region_21.22 | all-reduce | flops 3 | bytes 24 | tf_op jit(solution)/shard_map/psum | solution.py:162
  (404 shorter events, 63.0 us)
Async XLA Ops:
  0.6 22.7 %copy-start.6 = (s32[1024]{0:T(1024)S(1)}, s32[1024]{0:T(1024)}, u32[]{:S(2)}) copy-start(s32[1024]{0:T(1024)} %param.15) | copy-start | bytes 12292
  0.6 22.7 %copy-start.8 = (s32[1024]{0:T(1024)S(1)}, s32[1024]{0:T(1024)}, u32[]{:S(2)}) copy-start(s32[1024]{0:T(1024)} %param.16) | copy-start | bytes 12292
  12.3 11.1 %copy-start.7 = (s32[1024,1]{0,1:T(1,128)}, s32[1024,1]{0,1:T(1,128)S(1)}, u32[]{:S(2)}) copy-start(s32[1024,1]{0,1:T(1,128)S(1)} %compare_select_fusion.1) | copy-start | bytes 12292
  17.3 71.0 %all-to-all-start = ((s32[1,32,128]{2,0,1:T(1,128)}), s32[1,32,128]{2,0,1:T(1,128)S(1)}, u32[]{:S(2)}, u32[]{:S(2)}) async-start(s32[1,32,128]{2,0,1:T(1,128)} %bitcast.6), calls=%async_computation | async-start | bytes 32768 | tf_op jit(solution)/shard_map/all_to_all | solution.py:140
  23.4 4.6 copy-start.3
  23.4 4.6 copy-start.4
  46.8 3.7 copy-start
  49.1 1.4 copy-start.1
  88.3 35.6 %all-to-all-start.1 = ((f32[32,81,1,128]{3,2,1,0:T(1,128)}), f32[32,81,1,128]{3,2,1,0:T(1,128)S(1)}, u32[]{:S(2)}, u32[]{:S(2)}) async-start(f32[32,81,1,128]{3,2,1,0:T(1,128)} %constant_dynamic-update-slice_fusion), calls=%async_computation.1 | async-start | bytes 2654208 | tf_op jit(solution)/shard_map/all_to_all | solution.py:126
  166.2 3.7 collective-permute-start
  170.3 3.3 collective-permute-start.1
  173.8 4.6 collective-permute-start.2
  178.6 1.6 collective-permute-start.3
  186.4 0.7 copy-start.2
  186.8 2.0 copy-start.5
  200.6 3.7 collective-permute-start.4
  204.7 3.3 collective-permute-start.5
  292.8 4.6 collective-permute-start.6
  297.5 1.8 collective-permute-start.7
  319.7 3.7 collective-permute-start.8
  323.7 3.3 collective-permute-start.9
  409.8 4.6 collective-permute-start.10
  414.5 1.8 collective-permute-start.11
  436.7 3.7 collective-permute-start.12
  440.7 3.3 collective-permute-start.13
  526.4 4.6 collective-permute-start.14
  531.2 1.9 collective-permute-start.15
  553.4 3.7 collective-permute-start.16
  557.4 3.3 collective-permute-start.17
